TPU v7x, 32 devices: a whole 2x2x4 slice. The times are simulated.
32 devices in a mesh: replica: 2 (over core), shard: 16 (over z, y, x).
Axes of the slice: x: 2, y: 2, z: 4, core: 2. Of those that a mesh axis runs over, the one named last changes fastest.
Arguments:
- gradients: bfloat16 [2, 2, 16, 1024, 256], P('replica', None, None, 'shard'), may hold values from -36 to 36
- momentum: float32 [2, 16, 1024, 256], P('replica', None, 'shard'), may hold values from -3 to 3
- params: float32 [16, 1024, 256], P(None, ('shard', 'replica')), may hold values from -6 to 6
- outer_moment: float32 [16, 1024, 256], P(None, ('shard', 'replica')), may hold values from -2 to 2
- shadow: float32 [16, 1024, 256], P(None, ('shard', 'replica')), may hold values from -6 to 6
Outputs:
- new_params: float32 [16, 1024, 256], P(None, ('shard', 'replica'))
- new_outer_moment: float32 [16, 1024, 256], P(None, ('shard', 'replica'))
- new_shadow: float32 [16, 1024, 256], P(None, ('shard', 'replica'))
- new_momentum: float32 [2, 16, 1024, 256], P('replica', None, 'shard')
All inputs are finite; a program needn't handle non-finite values.
Results may differ from a plain program's by a relative error of at most 0.0085.
Values may be sent and summed in bfloat16 or wider, within the bound.
No kernel may reach another device: no remote copies, remote signals or barrier semaphores. Data moves between devices by JAX's collectives and lax.ppermute only.
A program may use at most 64 MiB of HBM per device.

v0:
```python
import math
import jax
import jax.numpy as jnp
from jax import lax
from jax.sharding import PartitionSpec as P

NS_ITERS = 5
quintic_a = 3.4445
quintic_b = -4.775
quintic_c = 2.0315
inner_beta = 0.95
outer_mu = 0.9
outer_rate = 0.7
shadow_decay = 0.9


def newton_schulz(block):
    squares = jnp.sum(jnp.square(block.astype(jnp.float32)))
    current = (block.astype(jnp.float32) / (jnp.sqrt(squares) + 1e-07)).astype(jnp.bfloat16)
    for _ in range(NS_ITERS):
        gram = jnp.einsum("di,dj->ij", current, current, preferred_element_type=jnp.float32).astype(
            jnp.bfloat16
        )
        square = jnp.dot(gram, gram, preferred_element_type=jnp.float32)
        poly = (quintic_b * gram.astype(jnp.float32) + quintic_c * square).astype(jnp.bfloat16)
        product = jnp.dot(current, poly, preferred_element_type=jnp.float32)
        current = (quintic_a * current.astype(jnp.float32) + product).astype(jnp.bfloat16)
    return current


def body(gradients, momentum, params, outer_moment, shadow):
    shards = lax.axis_size("shard")
    replicas = lax.axis_size("replica")
    _, inner, mats, rows, width = gradients.shape
    owned = mats // shards
    total_rows = rows * shards
    rows_each = rows // replicas
    scale_step = 0.2 * math.sqrt(total_rows)
    moment = momentum[0]
    updates = []
    for k in range(inner):
        grad = gradients[0, k].astype(jnp.float32)
        moment = inner_beta * moment + grad
        updates.append((grad + inner_beta * moment).astype(jnp.bfloat16))
    stacked = jnp.stack(updates, axis=1)
    moved = lax.all_to_all(stacked, "shard", split_axis=0, concat_axis=0, tiled=True)
    moved = moved.reshape((shards, owned, inner, rows, width))
    totals = []
    for m in range(owned):
        total = None
        for k in range(inner):
            ortho = newton_schulz(moved[:, m, k].reshape((total_rows, width)))
            term = scale_step * ortho.astype(jnp.float32)
            total = term if total is None else total + term
        totals.append(total)
    total = jnp.stack(totals).reshape((owned, shards, replicas, rows_each, width))
    me = lax.axis_index("replica")
    summed = lax.dynamic_index_in_dim(total, me, 2, keepdims=False)
    for step in range(1, replicas):
        theirs = lax.dynamic_index_in_dim(total, (me + step) % replicas, 2, keepdims=False)
        got = lax.ppermute(
            theirs.astype(jnp.bfloat16),
            "replica",
            [(i, (i + step) % replicas) for i in range(replicas)],
        )
        summed = summed + got.astype(jnp.float32)
    placed = lax.all_to_all(
        summed.astype(jnp.bfloat16), "shard", split_axis=1, concat_axis=0, tiled=True
    )
    outer_delta = placed.reshape((mats, rows_each, width)).astype(jnp.float32) / replicas
    new_outer = outer_mu * outer_moment + outer_delta
    new_params = params - outer_rate * (outer_delta + outer_mu * new_outer)
    new_shadow = shadow_decay * shadow + (1.0 - shadow_decay) * new_params
    return (new_params, new_outer, new_shadow, moment[None])


def solution(mesh):
    rows = P(None, ("shard", "replica"), None)
    mine = P("replica", None, "shard", None)
    return jax.shard_map(
        body,
        mesh=mesh,
        in_specs=(P("replica", None, None, "shard", None), mine, rows, rows, rows),
        out_specs=(rows, rows, rows, mine),
        check_vma=False,
    )
```

profile of v0, /device:TPU:0, one launch (start us, length us, event | category | flops | bytes accessed | tf_op | source)
XLA Modules:
  0.0 83.9 jit_solution(12345464679178923116)
XLA Ops:
  0.7 2.0 %fusion.51 = bf16[16,1,64,256]{3,2,1,0:T(8,128)(2,1)S(1)} fusion(f32[1,16,64,256]{3,2,1,0:T(8,128)} %param.6, bf16[1,2,16,64,256]{4,3,2,1,0:T(8,128)(2,1)} %param.5), kind=kLoop, calls=%fused_computation.89 | loop fusion | flops 2359296 | bytes 2621440 | tf_op jit(solution)/shard_map/convert_element_type | solution.py:44
  3.0 1.1 %pad_maximum_fusion = bf16[16,2,64,256]{3,2,1,0:T(8,128)(2,1)} fusion(bf16[16,1,64,256]{3,2,1,0:T(8,128)(2,1)S(1)} %fusion.51, bf16[16,1,64,256]{3,2,1,0:T(8,128)(2,1)S(1)} %fusion.52), kind=kLoop, calls=%fused_computation.90 | loop fusion | flops 524288 | bytes 2097152 | tf_op jit(solution)/shard_map/stack | solution.py:45
  4.1 8.4 %all-to-all-start = ((bf16[16,2,64,256]{3,2,1,0:T(8,128)(2,1)}), bf16[16,2,64,256]{3,2,1,0:T(8,128)(2,1)}, u32[]{:S(2)}, u32[]{:S(2)}) async-start(bf16[16,2,64,256]{3,2,1,0:T(8,128)(2,1)} %pad_maximum_fusion), calls=%async_computation | async-start | bytes 2097152 | tf_op jit(solution)/shard_map/all_to_all | solution.py:46
  12.5 24.4 %all-to-all-done = bf16[16,2,64,256]{3,2,1,0:T(8,128)(2,1)} async-done(((bf16[16,2,64,256]{3,2,1,0:T(8,128)(2,1)}), bf16[16,2,64,256]{3,2,1,0:T(8,128)(2,1)}, u32[]{:S(2)}, u32[]{:S(2)}) %all-to-all-start) | async-done | bytes 1048608 | tf_op jit(solution)/shard_map/all_to_all | solution.py:46
  36.9 1.3 %copy.17 = bf16[16,2,64,256]{3,2,0,1:T(8,128)(2,1)S(1)} copy(bf16[16,2,64,256]{3,2,1,0:T(8,128)(2,1)} %all-to-all-done) | data formatting | bytes 2097152 | tf_op jit(solution)/shard_map/all_to_all | solution.py:46
  38.2 0.9 %fusion.40 = (f32[]{:T(128)}, f32[]{:T(128)}) fusion(bf16[16,1,2,64,256]{4,3,0,2,1:T(8,128)(2,1)S(1)} %bitcast.151), kind=kLoop, calls=%fused_computation.78 | loop fusion | flops 1572862 | bytes 1048584 | tf_op jit(solution)/shard_map/reduce_sum | solution.py:18
  40.5 1.0 %fusion.41 = (bf16[16,1,1,64,256]{4,3,0,2,1:T(8,128)(2,1)S(1)}, bf16[16,1,1,64,256]{4,3,0,2,1:T(8,128)(2,1)}) fusion(f32[]{:T(128)S(6)} %add.149, bf16[16,1,2,64,256]{4,3,0,2,1:T(8,128)(2,1)S(1)} %bitcast.152, f32[]{:T(128)S(6)} %add.160), kind=kLoop, calls=%fused_computation.79 | loop fusion | flops 1572864 | bytes 2097160 | tf_op jit(solution)/shard_map/convert_element_type | solution.py:19
  42.3 1.7 %fusion.4 = bf16[1024,256]{1,0:T(8,128)(2,1)S(1)} fusion(bf16[1024,256]{1,0:T(8,128)(2,1)} %bitcast.156, bf16[256,256]{1,0:T(8,128)(2,1)S(1)} %fusion.28), kind=kOutput, calls=%fused_computation.22 | convolution fusion | flops 169148416 | bytes 1179648 | tf_op jit(solution)/shard_map/dot_general | solution.py:26
  45.3 0.5 fusion.6
  45.8 0.8 copy-done.8
  46.9 1.7 %fusion.7 = bf16[1024,256]{1,0:T(8,128)(2,1)S(1)} fusion(bf16[1024,256]{1,0:T(8,128)(2,1)} %copy-done.8, bf16[256,256]{1,0:T(8,128)(2,1)S(1)} %convolution_convert_fusion.5), kind=kOutput, calls=%fused_computation.25 | convolution fusion | flops 169148416 | bytes 1179648 | tf_op jit(solution)/shard_map/dot_general | solution.py:26
  51.1 0.5 fusion.13
  52.6 0.8 copy-done.9
  53.7 1.7 %fusion.15 = bf16[1024,256]{1,0:T(8,128)(2,1)S(1)} fusion(bf16[1024,256]{1,0:T(8,128)(2,1)} %copy-done.9, bf16[256,256]{1,0:T(8,128)(2,1)S(1)} %convolution_convert_fusion.1), kind=kOutput, calls=%fused_computation.33 | convolution fusion | flops 169148416 | bytes 1179648 | tf_op jit(solution)/shard_map/dot_general | solution.py:26
  55.4 0.8 copy-done.2
  56.6 1.7 %fusion.17 = f32[1024,256]{1,0:T(8,128)S(1)} fusion(bf16[1024,256]{1,0:T(8,128)(2,1)} %copy-done.2, bf16[256,256]{1,0:T(8,128)(2,1)S(1)} %convolution_convert_fusion), kind=kOutput, calls=%fused_computation.35 | convolution fusion | flops 169410560 | bytes 1703936 | tf_op jit(solution)/shard_map/dot_general | solution.py:26
  58.3 2.7 %fusion.11 = f32[1024,256]{1,0:T(8,128)} fusion(f32[1024,256]{1,0:T(8,128)S(1)} %fusion.17, bf16[1024,256]{1,0:T(8,128)(2,1)} %copy-done.5, bf16[256,256]{1,0:T(8,128)(2,1)S(1)} %convolution_convert_fusion.4), kind=kOutput, calls=%fused_computation.29 | convolution fusion | flops 169934848 | bytes 2752512 | tf_op jit(solution)/shard_map/dot_general | solution.py:26
  61.0 1.1 %fusion.58 = bf16[1,16,32,256]{3,2,0,1:T(8,128)(2,1)S(1)} fusion(f32[1,16,2,32,256]{4,3,2,1,0:T(8,128)} %bitcast.153, s32[]{:T(128)S(6)} %select_n.16), kind=kLoop, calls=%fused_computation.104 | loop fusion | bytes 524292 | tf_op jit(solution)/shard_map/convert_element_type | solution.py:62
  62.1 1.5 %collective-permute-done = bf16[1,16,32,256]{3,2,0,1:T(8,128)(2,1)S(1)} collective-permute-done((bf16[1,16,32,256]{3,2,0,1:T(8,128)(2,1)S(1)}, bf16[1,16,32,256]{3,2,0,1:T(8,128)(2,1)S(1)}, u32[]{:S(2)}, u32[]{:S(2)}) %collective-permute-start) | collective-permute-done | bytes 262176 | tf_op jit(solution)/shard_map/ppermute | solution.py:61
  63.7 1.8 %fusion.55 = bf16[1,16,32,256]{3,2,0,1:T(8,128)(2,1)} fusion(bf16[1,16,32,256]{3,2,0,1:T(8,128)(2,1)S(1)} %collective-permute-done, f32[1,16,2,32,256]{4,3,2,1,0:T(8,128)} %bitcast.154, s32[]{:T(128)S(6)} %select_n.14), kind=kLoop, calls=%fused_computation.99 | loop fusion | flops 393216 | bytes 1048580 | tf_op jit(solution)/shard_map/convert_element_type | solution.py:68
  65.5 5.9 %all-to-all-start.1 = ((bf16[1,16,32,256]{3,2,0,1:T(8,128)(2,1)}), bf16[1,16,32,256]{3,2,0,1:T(8,128)(2,1)S(1)}, u32[]{:S(2)}, u32[]{:S(2)}) async-start(bf16[1,16,32,256]{3,2,0,1:T(8,128)(2,1)} %fusion.55), calls=%async_computation.1 | async-start | bytes 524288 | tf_op jit(solution)/shard_map/all_to_all | solution.py:67
  71.4 1.2 %fusion.49 = f32[1,16,64,256]{3,2,1,0:T(8,128)} fusion(f32[1,16,64,256]{3,2,1,0:T(8,128)S(1)} %copy-done, bf16[1,2,16,64,256]{4,3,2,1,0:T(8,128)(2,1)S(1)} %copy-done.1), kind=kLoop, calls=%fused_computation.87 | loop fusion | flops 1572864 | bytes 3145728 | tf_op jit(solution)/shard_map/add | solution.py:43
  72.6 8.9 %all-to-all-done.1 = bf16[1,16,32,256]{3,2,0,1:T(8,128)(2,1)S(1)} async-done(((bf16[1,16,32,256]{3,2,0,1:T(8,128)(2,1)}), bf16[1,16,32,256]{3,2,0,1:T(8,128)(2,1)S(1)}, u32[]{:S(2)}, u32[]{:S(2)}) %all-to-all-start.1) | async-done | bytes 262176 | tf_op jit(solution)/shard_map/all_to_all | solution.py:67
  81.5 2.4 %multiply_add_fusion = (f32[16,32,256]{2,1,0:T(8,128)}, f32[16,32,256]{2,1,0:T(8,128)}, f32[16,32,256]{2,1,0:T(8,128)}) fusion(f32[16,32,256]{2,1,0:T(8,128)S(1)} %copy-done.3, f32[16,32,256]{2,1,0:T(8,128)S(1)} %copy-done.4, bf16[1,16,32,256]{3,2,0,1:T(8,128)(2,1)S(1)} %all-to-all-done.1, f32[16,32,256]{2,1,0:T(8,128)} %param.8), kind=kLoop, calls=%fused_computation.102 | loop fusion | flops 1441792 | bytes 3407872 | tf_op jit(solution)/shard_map/add | solution.py:73
  (32 shorter events, 6.8 us)
Async XLA Ops:
  0.6 2.0 %copy-start.1 = (bf16[1,2,16,64,256]{4,3,2,1,0:T(8,128)(2,1)S(1)}, bf16[1,2,16,64,256]{4,3,2,1,0:T(8,128)(2,1)}, u32[]{:S(2)}) copy-start(bf16[1,2,16,64,256]{4,3,2,1,0:T(8,128)(2,1)} %param.5) | copy-start | bytes 3145732
  0.6 2.2 %copy-start = (f32[1,16,64,256]{3,2,1,0:T(8,128)S(1)}, f32[1,16,64,256]{3,2,1,0:T(8,128)}, u32[]{:S(2)}) copy-start(f32[1,16,64,256]{3,2,1,0:T(8,128)} %param.6) | copy-start | bytes 3145732
  4.1 32.8 %all-to-all-start = ((bf16[16,2,64,256]{3,2,1,0:T(8,128)(2,1)}), bf16[16,2,64,256]{3,2,1,0:T(8,128)(2,1)}, u32[]{:S(2)}, u32[]{:S(2)}) async-start(bf16[16,2,64,256]{3,2,1,0:T(8,128)(2,1)} %pad_maximum_fusion), calls=%async_computation | async-start | bytes 2097152 | tf_op jit(solution)/shard_map/all_to_all | solution.py:46
  41.5 0.8 copy-start.7
  45.8 0.8 copy-start.8
  48.7 0.8 copy-start.5
  48.7 1.2 %copy-start.6 = (bf16[16,1,1,64,256]{4,3,0,2,1:T(8,128)(2,1)S(1)}, bf16[16,1,1,64,256]{4,3,0,2,1:T(8,128)(2,1)}, u32[]{:S(2)}) copy-start(bf16[16,1,1,64,256]{4,3,0,2,1:T(8,128)(2,1)} %get-tuple-element.10) | copy-start | bytes 1572868
  52.5 0.8 copy-start.9
  55.4 0.8 copy-start.2
  62.1 1.6 %collective-permute-start = (bf16[1,16,32,256]{3,2,0,1:T(8,128)(2,1)S(1)}, bf16[1,16,32,256]{3,2,0,1:T(8,128)(2,1)S(1)}, u32[]{:S(2)}, u32[]{:S(2)}) collective-permute-start(bf16[1,16,32,256]{3,2,0,1:T(8,128)(2,1)S(1)} %fusion.58), channel_id=1, source_target_pairs={{0,16},{16,0},{1,17},{17,1},{2,18},{18,2},{3,19},{19,3},{4,20},{20... | collective-permute-start | bytes 786440 | tf_op jit(solution)/shard_map/ppermute | solution.py:61
  65.5 16.0 %all-to-all-start.1 = ((bf16[1,16,32,256]{3,2,0,1:T(8,128)(2,1)}), bf16[1,16,32,256]{3,2,0,1:T(8,128)(2,1)S(1)}, u32[]{:S(2)}, u32[]{:S(2)}) async-start(bf16[1,16,32,256]{3,2,0,1:T(8,128)(2,1)} %fusion.55), calls=%async_computation.1 | async-start | bytes 524288 | tf_op jit(solution)/shard_map/all_to_all | solution.py:67
  71.4 10.2 %copy-start.3 = (f32[16,32,256]{2,1,0:T(8,128)S(1)}, f32[16,32,256]{2,1,0:T(8,128)}, u32[]{:S(2)}) copy-start(f32[16,32,256]{2,1,0:T(8,128)} %param.9) | copy-start | bytes 1572868
  71.4 10.2 %copy-start.4 = (f32[16,32,256]{2,1,0:T(8,128)S(1)}, f32[16,32,256]{2,1,0:T(8,128)}, u32[]{:S(2)}) copy-start(f32[16,32,256]{2,1,0:T(8,128)} %param.7) | copy-start | bytes 1572868
where the time goes:
time: 84.5 us; the launch traced here: 83.9 us
  waiting for transfers between devices  34.9 us (41%)
  matrix products  15.6 us (18%)
  starting transfers between devices  14.3 us (17%)
  other arithmetic  10.5 us (12%)
  local copies, waits for them, and re-layouts  6.24 us (7%)
  between operations  2.27 us (3%)
    all_to_all x1, waiting for transfers between devices, body(): lax.all_to_all(stacked, 'shard', split_axis=0, concat_axis=0, tiled=True)  24.4 us
    dot_general x10, matrix products, newton_schulz(): product = jnp.dot(current, poly, preferred_element_type=jnp.float32)  12.2 us
    all_to_all x1, waiting for transfers between devices, body(): lax.all_to_all(summed.astype(jnp.bfloat16), 'shard', split_axis=1, concat...  8.93 us
    all_to_all x1, starting transfers between devices, body(): lax.all_to_all(stacked, 'shard', split_axis=0, concat_axis=0, tiled=True)  8.39 us
    all_to_all x1, starting transfers between devices, body(): lax.all_to_all(summed.astype(jnp.bfloat16), 'shard', split_axis=1, concat...  5.86 us
    unnamed x20, local copies, waits for them, and re-layouts  3.88 us
    dot_general x10, matrix products, newton_schulz(): jnp.einsum('di,dj->ij', current, current, preferred_element_type=jnp.floa...  3.45 us
    add x1, other arithmetic, body(): new_shadow = shadow_decay * shadow + (1.0 - shadow_decay) * new_params  2.35 us
  transfers between devices with their start and end apart: 3, of which 3 were waited for; matrix products, arithmetic and copies ran while one was open for 1% of the time, Pallas kernels for 0%

commit v1 on v0

--- a/solution.py
+++ b/solution.py
@@ -64,8 +64,14 @@
             [(i, (i + step) % replicas) for i in range(replicas)],
         )
         summed = summed + got.astype(jnp.float32)
-    placed = lax.all_to_all(
-        summed.astype(jnp.bfloat16), "shard", split_axis=1, concat_axis=0, tiled=True
+    placed = jnp.concatenate(
+        lax.all_to_all(
+            jnp.stack(jnp.split(summed.astype(jnp.bfloat16), lax.axis_size("shard"), axis=1)),
+            "shard",
+            0,
+            0,
+        ),
+        axis=0,
     )
     outer_delta = placed.reshape((mats, rows_each, width)).astype(jnp.float32) / replicas
     new_outer = outer_mu * outer_moment + outer_delta

time: 84.5 us -> 93.5 us (1.11)
  local copies, waits for them, and re-layouts: 6.24 us -> 15.9 us
    unnamed x20 -> x35, local copies, waits for them, and re-layouts: 3.88 us -> 13 us
where the time goes in v1:
time: 93.5 us; the launch traced here: 92.9 us
  waiting for transfers between devices  34.9 us (37%)
  local copies, waits for them, and re-layouts  15.9 us (17%)
  matrix products  15.6 us (17%)
  starting transfers between devices  14.3 us (15%)
  other arithmetic  9.84 us (11%)
  between operations  2.29 us (2%)
    all_to_all x1, waiting for transfers between devices, body(): lax.all_to_all(stacked, 'shard', split_axis=0, concat_axis=0, tiled=True)  24.4 us
    unnamed x35, local copies, waits for them, and re-layouts  13 us
    dot_general x10, matrix products, newton_schulz(): product = jnp.dot(current, poly, preferred_element_type=jnp.float32)  12.2 us
    all_to_all x1, waiting for transfers between devices, body(): lax.all_to_all(jnp.stack(jnp.split(summed.astype(jnp.bfloat16), lax.axis_...  8.93 us
    all_to_all x1, starting transfers between devices, body(): lax.all_to_all(stacked, 'shard', split_axis=0, concat_axis=0, tiled=True)  8.39 us
    all_to_all x1, starting transfers between devices, body(): lax.all_to_all(jnp.stack(jnp.split(summed.astype(jnp.bfloat16), lax.axis_...  5.86 us
    dot_general x10, matrix products, newton_schulz(): jnp.einsum('di,dj->ij', current, current, preferred_element_type=jnp.floa...  3.45 us
    add x1, other arithmetic, body(): new_shadow = shadow_decay * shadow + (1.0 - shadow_decay) * new_params  2.35 us
  transfers between devices with their start and end apart: 3, of which 3 were waited for; matrix products, arithmetic and copies ran while one was open for 1% of the time, Pallas kernels for 0%

profile of v1, /device:TPU:0, one launch (start us, length us, event | category | flops | bytes accessed | tf_op | source)
XLA Modules:
  0.0 92.9 jit_solution(14557349139552856981)
XLA Ops:
  0.7 2.0 %fusion.51 = bf16[16,1,64,256]{3,2,1,0:T(8,128)(2,1)S(1)} fusion(f32[1,16,64,256]{3,2,1,0:T(8,128)} %param.6, bf16[1,2,16,64,256]{4,3,2,1,0:T(8,128)(2,1)} %param.5), kind=kLoop, calls=%fused_computation.89 | loop fusion | flops 2359296 | bytes 2621440 | tf_op jit(solution)/shard_map/convert_element_type | solution.py:44
  3.0 1.1 %pad_maximum_fusion = bf16[16,2,64,256]{3,2,1,0:T(8,128)(2,1)} fusion(bf16[16,1,64,256]{3,2,1,0:T(8,128)(2,1)S(1)} %fusion.51, bf16[16,1,64,256]{3,2,1,0:T(8,128)(2,1)S(1)} %fusion.52), kind=kLoop, calls=%fused_computation.90 | loop fusion | flops 524288 | bytes 2097152 | tf_op jit(solution)/shard_map/stack | solution.py:45
  4.1 8.4 %all-to-all-start = ((bf16[16,2,64,256]{3,2,1,0:T(8,128)(2,1)}), bf16[16,2,64,256]{3,2,1,0:T(8,128)(2,1)}, u32[]{:S(2)}, u32[]{:S(2)}) async-start(bf16[16,2,64,256]{3,2,1,0:T(8,128)(2,1)} %pad_maximum_fusion), calls=%async_computation | async-start | bytes 2097152 | tf_op jit(solution)/shard_map/all_to_all | solution.py:46
  12.5 24.4 %all-to-all-done = bf16[16,2,64,256]{3,2,1,0:T(8,128)(2,1)} async-done(((bf16[16,2,64,256]{3,2,1,0:T(8,128)(2,1)}), bf16[16,2,64,256]{3,2,1,0:T(8,128)(2,1)}, u32[]{:S(2)}, u32[]{:S(2)}) %all-to-all-start) | async-done | bytes 1048608 | tf_op jit(solution)/shard_map/all_to_all | solution.py:46
  36.9 1.3 %copy.32 = bf16[16,2,64,256]{3,2,0,1:T(8,128)(2,1)S(1)} copy(bf16[16,2,64,256]{3,2,1,0:T(8,128)(2,1)} %all-to-all-done) | data formatting | bytes 2097152 | tf_op jit(solution)/shard_map/all_to_all | solution.py:46
  38.2 0.9 fusion.40
  40.5 1.0 %fusion.41 = (bf16[16,1,1,64,256]{4,3,0,2,1:T(8,128)(2,1)S(1)}, bf16[16,1,1,64,256]{4,3,0,2,1:T(8,128)(2,1)}) fusion(f32[]{:T(128)S(6)} %add.149, bf16[16,1,2,64,256]{4,3,0,2,1:T(8,128)(2,1)S(1)} %bitcast.216, f32[]{:T(128)S(6)} %add.160), kind=kLoop, calls=%fused_computation.79 | loop fusion | flops 1572864 | bytes 2097160 | tf_op jit(solution)/shard_map/convert_element_type | solution.py:19
  42.3 1.7 %fusion.4 = bf16[1024,256]{1,0:T(8,128)(2,1)S(1)} fusion(bf16[1024,256]{1,0:T(8,128)(2,1)} %bitcast.220, bf16[256,256]{1,0:T(8,128)(2,1)S(1)} %fusion.28), kind=kOutput, calls=%fused_computation.22 | convolution fusion | flops 169148416 | bytes 1179648 | tf_op jit(solution)/shard_map/dot_general | solution.py:26
  45.8 0.8 copy-done.8
  46.9 1.7 %fusion.7 = bf16[1024,256]{1,0:T(8,128)(2,1)S(1)} fusion(bf16[1024,256]{1,0:T(8,128)(2,1)} %copy-done.8, bf16[256,256]{1,0:T(8,128)(2,1)S(1)} %convolution_convert_fusion.5), kind=kOutput, calls=%fused_computation.25 | convolution fusion | flops 169148416 | bytes 1179648 | tf_op jit(solution)/shard_map/dot_general | solution.py:26
  52.6 0.8 copy-done.9
  53.7 1.7 %fusion.15 = bf16[1024,256]{1,0:T(8,128)(2,1)S(1)} fusion(bf16[1024,256]{1,0:T(8,128)(2,1)} %copy-done.9, bf16[256,256]{1,0:T(8,128)(2,1)S(1)} %convolution_convert_fusion.1), kind=kOutput, calls=%fused_computation.33 | convolution fusion | flops 169148416 | bytes 1179648 | tf_op jit(solution)/shard_map/dot_general | solution.py:26
  55.4 0.8 copy-done.2
  56.6 1.7 %fusion.17 = f32[1024,256]{1,0:T(8,128)S(1)} fusion(bf16[1024,256]{1,0:T(8,128)(2,1)} %copy-done.2, bf16[256,256]{1,0:T(8,128)(2,1)S(1)} %convolution_convert_fusion), kind=kOutput, calls=%fused_computation.35 | convolution fusion | flops 169410560 | bytes 1703936 | tf_op jit(solution)/shard_map/dot_general | solution.py:26
  58.3 2.7 %fusion.11 = f32[1024,256]{1,0:T(8,128)} fusion(f32[1024,256]{1,0:T(8,128)S(1)} %fusion.17, bf16[1024,256]{1,0:T(8,128)(2,1)} %copy-done.5, bf16[256,256]{1,0:T(8,128)(2,1)S(1)} %convolution_convert_fusion.4), kind=kOutput, calls=%fused_computation.29 | convolution fusion | flops 169934848 | bytes 2752512 | tf_op jit(solution)/shard_map/dot_general | solution.py:26
  61.0 1.1 %fusion.58 = bf16[1,16,32,256]{3,2,1,0:T(8,128)(2,1)S(1)} fusion(f32[1,16,2,32,256]{4,3,2,1,0:T(8,128)} %bitcast.217, s32[]{:T(128)S(6)} %select_n.16), kind=kLoop, calls=%fused_computation.104 | loop fusion | bytes 524292 | tf_op jit(solution)/shard_map/convert_element_type | solution.py:62
  62.1 1.5 %collective-permute-done = bf16[1,16,32,256]{3,2,1,0:T(8,128)(2,1)S(1)} collective-permute-done((bf16[1,16,32,256]{3,2,1,0:T(8,128)(2,1)S(1)}, bf16[1,16,32,256]{3,2,1,0:T(8,128)(2,1)S(1)}, u32[]{:S(2)}, u32[]{:S(2)}) %collective-permute-start) | collective-permute-done | bytes 262176 | tf_op jit(solution)/shard_map/ppermute | solution.py:61
  63.7 1.1 %fusion.55 = bf16[1,16,32,256]{3,2,1,0:T(8,128)(2,1)S(1)} fusion(bf16[1,16,32,256]{3,2,1,0:T(8,128)(2,1)S(1)} %collective-permute-done, f32[1,16,2,32,256]{4,3,2,1,0:T(8,128)} %bitcast.218, s32[]{:T(128)S(6)} %select_n.14), kind=kLoop, calls=%fused_computation.99 | loop fusion | flops 393216 | bytes 1048580 | tf_op jit(solution)/shard_map/convert_element_type | solution.py:69
  64.8 0.6 constant_dynamic-update-slice_fusion.15
  65.4 0.6 constant_dynamic-update-slice_fusion.14
  74.5 5.9 %all-to-all-start.1 = ((bf16[16,1,1,32,256]{4,3,2,1,0:T(8,128)(2,1)}), bf16[16,1,1,32,256]{4,3,2,1,0:T(8,128)(2,1)S(1)}, u32[]{:S(2)}, u32[]{:S(2)}) async-start(bf16[16,1,1,32,256]{4,3,2,1,0:T(8,128)(2,1)} %constant_dynamic-update-slice_fusion), calls=%async_computation.1 | async-start | bytes 524288 | tf_op jit(solution)/shard_map/all_to_all | solution.py:68
  80.4 1.2 %fusion.49 = f32[1,16,64,256]{3,2,1,0:T(8,128)} fusion(f32[1,16,64,256]{3,2,1,0:T(8,128)S(1)} %copy-done, bf16[1,2,16,64,256]{4,3,2,1,0:T(8,128)(2,1)S(1)} %copy-done.1), kind=kLoop, calls=%fused_computation.87 | loop fusion | flops 1572864 | bytes 3145728 | tf_op jit(solution)/shard_map/add | solution.py:43
  81.6 8.9 %all-to-all-done.1 = bf16[16,1,1,32,256]{4,3,2,1,0:T(8,128)(2,1)S(1)} async-done(((bf16[16,1,1,32,256]{4,3,2,1,0:T(8,128)(2,1)}), bf16[16,1,1,32,256]{4,3,2,1,0:T(8,128)(2,1)S(1)}, u32[]{:S(2)}, u32[]{:S(2)}) %all-to-all-start.1) | async-done | bytes 262176 | tf_op jit(solution)/shard_map/all_to_all | solution.py:68
  90.5 2.4 %multiply_add_fusion = (f32[16,32,256]{2,1,0:T(8,128)}, f32[16,32,256]{2,1,0:T(8,128)}, f32[16,32,256]{2,1,0:T(8,128)}) fusion(f32[16,32,256]{2,1,0:T(8,128)S(1)} %copy-done.3, f32[16,32,256]{2,1,0:T(8,128)S(1)} %copy-done.4, bf16[16,1,1,32,256]{4,3,2,1,0:T(8,128)(2,1)S(1)} %all-to-all-done.1, f32[16,32,256]{2,1,0:T(8,128)} %param.8), kind=kLoop, calls=%fused_computation.102 | loop fusion | flops 1441792 | bytes 3407872 | tf_op jit(solution)/shard_map/add | solution.py:79
  (48 shorter events, 16.3 us)
Async XLA Ops:
  0.6 2.0 %copy-start.1 = (bf16[1,2,16,64,256]{4,3,2,1,0:T(8,128)(2,1)S(1)}, bf16[1,2,16,64,256]{4,3,2,1,0:T(8,128)(2,1)}, u32[]{:S(2)}) copy-start(bf16[1,2,16,64,256]{4,3,2,1,0:T(8,128)(2,1)} %param.5) | copy-start | bytes 3145732
  0.6 2.2 %copy-start = (f32[1,16,64,256]{3,2,1,0:T(8,128)S(1)}, f32[1,16,64,256]{3,2,1,0:T(8,128)}, u32[]{:S(2)}) copy-start(f32[1,16,64,256]{3,2,1,0:T(8,128)} %param.6) | copy-start | bytes 3145732
  4.1 32.8 %all-to-all-start = ((bf16[16,2,64,256]{3,2,1,0:T(8,128)(2,1)}), bf16[16,2,64,256]{3,2,1,0:T(8,128)(2,1)}, u32[]{:S(2)}, u32[]{:S(2)}) async-start(bf16[16,2,64,256]{3,2,1,0:T(8,128)(2,1)} %pad_maximum_fusion), calls=%async_computation | async-start | bytes 2097152 | tf_op jit(solution)/shard_map/all_to_all | solution.py:46
  41.5 0.8 copy-start.7
  45.8 0.8 copy-start.8
  48.7 0.8 copy-start.5
  48.7 1.2 %copy-start.6 = (bf16[16,1,1,64,256]{4,3,0,2,1:T(8,128)(2,1)S(1)}, bf16[16,1,1,64,256]{4,3,0,2,1:T(8,128)(2,1)}, u32[]{:S(2)}) copy-start(bf16[16,1,1,64,256]{4,3,0,2,1:T(8,128)(2,1)} %get-tuple-element.10) | copy-start | bytes 1572868
  52.5 0.8 copy-start.9
  55.4 0.8 copy-start.2
  62.1 1.6 %collective-permute-start = (bf16[1,16,32,256]{3,2,1,0:T(8,128)(2,1)S(1)}, bf16[1,16,32,256]{3,2,1,0:T(8,128)(2,1)S(1)}, u32[]{:S(2)}, u32[]{:S(2)}) collective-permute-start(bf16[1,16,32,256]{3,2,1,0:T(8,128)(2,1)S(1)} %fusion.58), channel_id=1, source_target_pairs={{0,16},{16,0},{1,17},{17,1},{2,18},{18,2},{3,19},{19,3},{4,20},{20... | collective-permute-start | bytes 786440 | tf_op jit(solution)/shard_map/ppermute | solution.py:61
  74.5 16.0 %all-to-all-start.1 = ((bf16[16,1,1,32,256]{4,3,2,1,0:T(8,128)(2,1)}), bf16[16,1,1,32,256]{4,3,2,1,0:T(8,128)(2,1)S(1)}, u32[]{:S(2)}, u32[]{:S(2)}) async-start(bf16[16,1,1,32,256]{4,3,2,1,0:T(8,128)(2,1)} %constant_dynamic-update-slice_fusion), calls=%async_computation.1 | async-start | bytes 524288 | tf_op jit(solution)/shard_map/all_to_all | solution.py:68
  80.4 10.2 %copy-start.3 = (f32[16,32,256]{2,1,0:T(8,128)S(1)}, f32[16,32,256]{2,1,0:T(8,128)}, u32[]{:S(2)}) copy-start(f32[16,32,256]{2,1,0:T(8,128)} %param.9) | copy-start | bytes 1572868
  80.4 10.2 %copy-start.4 = (f32[16,32,256]{2,1,0:T(8,128)S(1)}, f32[16,32,256]{2,1,0:T(8,128)}, u32[]{:S(2)}) copy-start(f32[16,32,256]{2,1,0:T(8,128)} %param.7) | copy-start | bytes 1572868
